TPU v7x, 32 devices: a whole 2x2x4 slice. The times are simulated.
32 devices in a mesh: grp: 2 (over core), ctx: 4 (over z), wsh: 4 (over y, x).
Axes of the slice: x: 2, y: 2, z: 4, core: 2. Of those that a mesh axis runs over, the one named last changes fastest.
Arguments:
- tokens: bfloat16 [6144, 1152], P(('grp', 'ctx', 'wsh')), may hold values from -6 to 6
- segment_ids: int32 [6144], P(('grp', 'ctx', 'wsh')), may hold values from 0 to 1, as said below
- positions: int32 [6144], P(('grp', 'ctx', 'wsh')), may hold values from 0 to 3071, as said below
- attend_gain: float32 [1152], replicated, may hold values from 0.5 to 1.5
- query_key_value: bfloat16 [1152, 1920], P('wsh'), may hold values from -0.25 to 0.25
- attend_out: bfloat16 [1152, 1152], P('wsh'), may hold values from -2 to 2
- feed_gain: float32 [1152], replicated, may hold values from 0.5 to 1.5
- gate_up: bfloat16 [1152, 6144], P('wsh'), may hold values from -0.1875 to 0.1875
- down_weight: bfloat16 [3072, 1152], P('wsh'), may hold values from -0.4375 to 0.4375
- upstream: bfloat16 [6144, 1152], P(('grp', 'ctx', 'wsh')), may hold values from -6 to 6
Outputs:
- activations: bfloat16 [6144, 1152], P(('grp', 'ctx', 'wsh'))
- input_grad: float32 [6144, 1152], P(('grp', 'ctx', 'wsh'))
- query_key_value_grad: float32 [1152, 1920], P(('ctx', 'wsh'))
- attend_out_grad: float32 [1152, 1152], P(('ctx', 'wsh'))
- gate_up_grad: float32 [1152, 6144], P(('ctx', 'wsh'))
- down_weight_grad: float32 [3072, 1152], P(('ctx', 'wsh'))
- attend_gain_grad: float32 [1152], P(('ctx', 'wsh'))
- feed_gain_grad: float32 [1152], P(('ctx', 'wsh'))
Inputs may be any that keep to these rules, and one draw needn't show every extreme that they name: `segment_ids`: in each group of 3072 rows the aligned runs of 96 rows are the runs of 96 consecutive tokens of that group's token stream, in some order, each once; the stream is the prompt of 2048 tokens (segment 0) followed by 1 continuations of 1024 tokens (segments 1 to 1). `positions`: matching segment_ids: a prompt token's position is its index in the prompt; a continuation token's position is 2048 plus its index in its continuation.
All inputs are finite; a program needn't handle non-finite values.
Results may differ from a plain program's by a relative error of at most 0.02.
Values may be sent and summed in bfloat16 or wider, within the bound.
A program may use at most 256 MiB of HBM per device.

v0:
```python
import math
import jax
import jax.numpy as jnp
from jax import lax
from jax.sharding import PartitionSpec as P

HEADS = 18
KV_HEADS = 6
HEAD_DIM = 64
FF = 3072
KTILE = 1024
QW = 1152
KW = 384
EPSILON = 1e-05


def rope_angles(positions):
    halfway = HEAD_DIM // 2
    frequency = jnp.exp(jnp.arange(halfway, dtype=jnp.float32) * (-math.log(10000.0) / halfway))
    angles = positions.astype(jnp.float32)[:, None] * frequency[None, :]
    return (jnp.cos(angles), jnp.sin(angles))


def rotate(tensor, cosine, sine_table):
    halfway = tensor.shape[-1] // 2
    first_half = tensor[..., :halfway]
    second_half = tensor[..., halfway:]
    cos_wide = cosine[:, None, :]
    sin_wide = sine_table[:, None, :]
    return jnp.concatenate(
        [
            first_half * cos_wide - second_half * sin_wide,
            second_half * cos_wide + first_half * sin_wide,
        ],
        axis=-1,
    )


def unrotate(gradient, cosine, sine_table):
    halfway = gradient.shape[-1] // 2
    first_half = gradient[..., :halfway]
    second_half = gradient[..., halfway:]
    cos_wide = cosine[:, None, :]
    sin_wide = sine_table[:, None, :]
    return jnp.concatenate(
        [
            first_half * cos_wide + second_half * sin_wide,
            second_half * cos_wide - first_half * sin_wide,
        ],
        axis=-1,
    )


def rms_factor(values):
    return lax.rsqrt(jnp.mean(values * values, axis=-1, keepdims=True) + EPSILON)


def norm_back(grad_normed, inputs, factor, gain):
    weighted = grad_normed * gain
    inner_mean = jnp.mean(weighted * inputs, axis=-1, keepdims=True)
    input_part = factor * weighted - inputs * (factor * factor * factor) * inner_mean
    return (input_part, jnp.sum(grad_normed * inputs * factor, axis=0))


def rounded(values):
    return lax.optimization_barrier(values.astype(jnp.bfloat16)).astype(jnp.float32)


def tile_mask(segment_ids, positions, seg_key, pos_key):
    return (pos_key[None, :] <= positions[:, None]) & (
        (seg_key[None, :] == 0) | (seg_key[None, :] == segment_ids[:, None])
    )


def tile_scores(queries, key_tile, allowed):
    raw_scores = jnp.einsum(
        "nhjd,khd->hjnk", queries, key_tile, preferred_element_type=jnp.float32
    ) * HEAD_DIM ** (-0.5)
    return jnp.where(allowed, raw_scores, -1e30)


def split_tiles(key_all, value_all, seg_all, pos_all):
    tile_count = key_all.shape[0] // KTILE
    key_tiles = key_all.reshape(tile_count, KTILE, KV_HEADS, HEAD_DIM)
    value_tiles = value_all.reshape(tile_count, KTILE, KV_HEADS, HEAD_DIM)
    return (
        key_tiles,
        value_tiles,
        seg_all.reshape(tile_count, KTILE),
        pos_all.reshape(tile_count, KTILE),
    )


def attend_forward(queries, key_all, value_all, seg_all, pos_all, segment_ids, positions):
    local_rows = queries.shape[0]
    head_ratio = HEADS // KV_HEADS
    key_tiles, value_tiles, seg_tiles, pos_tiles = split_tiles(key_all, value_all, seg_all, pos_all)

    def stats_step(state_pair, pieces):
        running_max, running_sum = state_pair
        key_tile, seg_key, pos_key = pieces
        allowed = tile_mask(segment_ids, positions, seg_key, pos_key)
        scores = tile_scores(queries, key_tile, allowed)
        new_max = jnp.maximum(running_max, jnp.max(scores, axis=-1))
        expons = jnp.where(allowed, jnp.exp(scores - new_max[..., None]), 0.0)
        new_sum = running_sum * jnp.exp(running_max - new_max) + jnp.sum(expons, axis=-1)
        return ((new_max, new_sum), None)

    start_max = jnp.full((KV_HEADS, head_ratio, local_rows), -1e30, jnp.float32)
    start_sum = jnp.zeros((KV_HEADS, head_ratio, local_rows), jnp.float32)
    (row_max, row_sum), _ = lax.scan(
        stats_step, (start_max, start_sum), (key_tiles, seg_tiles, pos_tiles)
    )
    log_total = row_max + jnp.log(row_sum)

    def value_step(running, pieces):
        key_tile, value_tile, seg_key, pos_key = pieces
        allowed = tile_mask(segment_ids, positions, seg_key, pos_key)
        scores = tile_scores(queries, key_tile, allowed)
        weights_tile = jnp.where(allowed, jnp.exp(scores - log_total[..., None]), 0.0).astype(
            jnp.bfloat16
        )
        return (
            running
            + jnp.einsum(
                "hjnk,khd->nhjd", weights_tile, value_tile, preferred_element_type=jnp.float32
            ),
            None,
        )

    start_out = jnp.zeros((local_rows, KV_HEADS, head_ratio, HEAD_DIM), jnp.float32)
    output, _ = lax.scan(value_step, start_out, (key_tiles, value_tiles, seg_tiles, pos_tiles))
    return (output, log_total)


def attend_backward(
    queries,
    key_all,
    value_all,
    seg_all,
    pos_all,
    segment_ids,
    positions,
    log_total,
    output_grad,
    output,
):
    key_count = key_all.shape[0]
    key_tiles, value_tiles, seg_tiles, pos_tiles = split_tiles(key_all, value_all, seg_all, pos_all)
    row_delta = jnp.einsum("nhjd,nhjd->hjn", output_grad.astype(jnp.float32), output)

    def grad_step(query_sum, pieces):
        key_tile, value_tile, seg_key, pos_key = pieces
        allowed = tile_mask(segment_ids, positions, seg_key, pos_key)
        scores = tile_scores(queries, key_tile, allowed)
        weights_tile = jnp.where(allowed, jnp.exp(scores - log_total[..., None]), 0.0)
        value_grad = jnp.einsum(
            "hjnk,nhjd->khd",
            weights_tile.astype(jnp.bfloat16),
            output_grad,
            preferred_element_type=jnp.float32,
        )
        weight_grad = jnp.einsum(
            "nhjd,khd->hjnk", output_grad, value_tile, preferred_element_type=jnp.float32
        )
        score_grad = (weights_tile * (weight_grad - row_delta[..., None])).astype(jnp.bfloat16)
        query_sum = query_sum + jnp.einsum(
            "hjnk,khd->nhjd", score_grad, key_tile, preferred_element_type=jnp.float32
        )
        key_grad = jnp.einsum(
            "hjnk,nhjd->khd", score_grad, queries, preferred_element_type=jnp.float32
        )
        return (query_sum, (key_grad, value_grad))

    start_query = jnp.zeros(queries.shape, jnp.float32)
    query_sum, (key_grads, value_grads) = lax.scan(
        grad_step, start_query, (key_tiles, value_tiles, seg_tiles, pos_tiles)
    )
    scale_factor = HEAD_DIM ** (-0.5)
    return (
        query_sum * scale_factor,
        key_grads.reshape(key_count, KW) * scale_factor,
        value_grads.reshape(key_count, KW),
    )


def local(
    tokens,
    segment_ids,
    positions,
    attend_gain,
    query_key_value,
    attend_out,
    feed_gain,
    gate_up,
    down_weight,
    upstream,
):
    local_rows = tokens.shape[0]
    head_ratio = HEADS // KV_HEADS
    inputs = tokens.astype(jnp.float32)
    factor_one = rms_factor(inputs)
    normed_one = (inputs * factor_one * attend_gain).astype(jnp.bfloat16)
    full_qkv, full_out, full_gate_up, full_down = (
        lax.all_gather(query_key_value, "wsh", axis=0, tiled=True),
        lax.all_gather(attend_out, "wsh", axis=0, tiled=True),
        lax.all_gather(gate_up, "wsh", axis=0, tiled=True),
        lax.all_gather(down_weight, "wsh", axis=0, tiled=True),
    )
    projected = jnp.dot(normed_one, full_qkv, preferred_element_type=jnp.float32)
    cosine, sine_table = rope_angles(positions)
    queries = rotate(
        projected[:, :QW].reshape(local_rows, HEADS, HEAD_DIM), cosine, sine_table
    ).astype(jnp.bfloat16)
    queries = queries.reshape(local_rows, KV_HEADS, head_ratio, HEAD_DIM)
    key_local = (
        rotate(
            projected[:, QW : QW + KW].reshape(local_rows, KV_HEADS, HEAD_DIM), cosine, sine_table
        )
        .astype(jnp.bfloat16)
        .reshape(local_rows, KW)
    )
    value_local = projected[:, QW + KW :].astype(jnp.bfloat16)
    key_all, value_all, seg_all, pos_all = (
        lax.all_gather(key_local, ("ctx", "wsh"), axis=0, tiled=True),
        lax.all_gather(value_local, ("ctx", "wsh"), axis=0, tiled=True),
        lax.all_gather(segment_ids, ("ctx", "wsh"), axis=0, tiled=True),
        lax.all_gather(positions, ("ctx", "wsh"), axis=0, tiled=True),
    )
    output, log_total = attend_forward(
        queries, key_all, value_all, seg_all, pos_all, segment_ids, positions
    )
    attended = output.reshape(local_rows, QW).astype(jnp.bfloat16)
    middle = inputs + jnp.dot(attended, full_out, preferred_element_type=jnp.float32)
    factor_two = rms_factor(middle)
    normed_two = (middle * factor_two * feed_gain).astype(jnp.bfloat16)
    gate_value = jnp.dot(normed_two, full_gate_up, preferred_element_type=jnp.float32)
    gate_part = gate_value[:, :FF]
    up_part = gate_value[:, FF:]
    sigmoid_gate = jax.nn.sigmoid(gate_part)
    silu_gate = gate_part * sigmoid_gate
    hidden = (silu_gate * up_part).astype(jnp.bfloat16)
    activations = (middle + jnp.dot(hidden, full_down, preferred_element_type=jnp.float32)).astype(
        jnp.bfloat16
    )
    back_qkv, back_out, back_gate_up, back_down = (
        lax.all_gather(query_key_value, "wsh", axis=0, tiled=True),
        lax.all_gather(attend_out, "wsh", axis=0, tiled=True),
        lax.all_gather(gate_up, "wsh", axis=0, tiled=True),
        lax.all_gather(down_weight, "wsh", axis=0, tiled=True),
    )
    down_grad = jnp.dot(hidden.T, upstream, preferred_element_type=jnp.float32)
    hidden_grad = jnp.dot(upstream, back_down.T, preferred_element_type=jnp.float32)
    gate_grad = hidden_grad * up_part * sigmoid_gate * (1.0 + gate_part * (1.0 - sigmoid_gate))
    up_grad = hidden_grad * silu_gate
    joint_grad = jnp.concatenate([gate_grad, up_grad], axis=1).astype(jnp.bfloat16)
    gate_up_grad = jnp.dot(normed_two.T, joint_grad, preferred_element_type=jnp.float32)
    normed_two_grad = jnp.dot(joint_grad, back_gate_up.T, preferred_element_type=jnp.float32)
    middle_part, feed_gain_grad = norm_back(normed_two_grad, middle, factor_two, feed_gain)
    middle_grad = upstream.astype(jnp.float32) + middle_part
    branch_grad = middle_grad.astype(jnp.bfloat16)
    out_weight_grad = jnp.dot(attended.T, branch_grad, preferred_element_type=jnp.float32)
    attended_grad = jnp.dot(branch_grad, back_out.T, preferred_element_type=jnp.float32).astype(
        jnp.bfloat16
    )
    attended_grad = attended_grad.reshape(local_rows, KV_HEADS, head_ratio, HEAD_DIM)
    query_grad, key_grad_all, value_grad_all = attend_backward(
        queries,
        key_all,
        value_all,
        seg_all,
        pos_all,
        segment_ids,
        positions,
        log_total,
        attended_grad,
        output,
    )
    key_grad, value_grad = (
        lax.psum_scatter(key_grad_all, ("ctx", "wsh"), scatter_dimension=0, tiled=True),
        lax.psum_scatter(value_grad_all, ("ctx", "wsh"), scatter_dimension=0, tiled=True),
    )
    query_back = unrotate(
        rounded(query_grad).reshape(local_rows, HEADS, HEAD_DIM), cosine, sine_table
    ).reshape(local_rows, QW)
    key_back = unrotate(
        rounded(key_grad).reshape(local_rows, KV_HEADS, HEAD_DIM), cosine, sine_table
    ).reshape(local_rows, KW)
    projected_grad = jnp.concatenate(
        [
            query_back.astype(jnp.bfloat16),
            key_back.astype(jnp.bfloat16),
            value_grad.astype(jnp.bfloat16),
        ],
        axis=1,
    )
    qkv_grad = jnp.dot(normed_one.T, projected_grad, preferred_element_type=jnp.float32)
    normed_one_grad = jnp.dot(projected_grad, back_qkv.T, preferred_element_type=jnp.float32)
    input_part, attend_gain_grad = norm_back(normed_one_grad, inputs, factor_one, attend_gain)
    input_grad = middle_grad + input_part
    shares = (
        lax.psum_scatter(qkv_grad, ("ctx", "wsh"), scatter_dimension=0, tiled=True),
        lax.psum_scatter(out_weight_grad, ("ctx", "wsh"), scatter_dimension=0, tiled=True),
        lax.psum_scatter(gate_up_grad, ("ctx", "wsh"), scatter_dimension=0, tiled=True),
        lax.psum_scatter(down_grad, ("ctx", "wsh"), scatter_dimension=0, tiled=True),
        lax.psum_scatter(attend_gain_grad, ("ctx", "wsh"), scatter_dimension=0, tiled=True),
        lax.psum_scatter(feed_gain_grad, ("ctx", "wsh"), scatter_dimension=0, tiled=True),
    )
    shares = (
        lax.psum(shares[0].astype(jnp.bfloat16), "grp").astype(jnp.float32),
        lax.psum(shares[1].astype(jnp.bfloat16), "grp").astype(jnp.float32),
        lax.psum(shares[2].astype(jnp.bfloat16), "grp").astype(jnp.float32),
        lax.psum(shares[3].astype(jnp.bfloat16), "grp").astype(jnp.float32),
        lax.psum(shares[4].astype(jnp.bfloat16), "grp").astype(jnp.float32),
        lax.psum(shares[5].astype(jnp.bfloat16), "grp").astype(jnp.float32),
    )
    return (
        activations,
        input_grad,
        shares[0],
        shares[1],
        shares[2],
        shares[3],
        shares[4],
        shares[5],
    )


def solution(mesh):
    in_specs = (
        P(("grp", "ctx", "wsh"), None),
        P(("grp", "ctx", "wsh")),
        P(("grp", "ctx", "wsh")),
        P(),
        P("wsh", None),
        P("wsh", None),
        P(),
        P("wsh", None),
        P("wsh", None),
        P(("grp", "ctx", "wsh"), None),
    )
    out_specs = (
        P(("grp", "ctx", "wsh"), None),
        P(("grp", "ctx", "wsh"), None),
        P(("ctx", "wsh"), None),
        P(("ctx", "wsh"), None),
        P(("ctx", "wsh"), None),
        P(("ctx", "wsh"), None),
        P(("ctx", "wsh")),
        P(("ctx", "wsh")),
    )
    return jax.shard_map(local, mesh=mesh, in_specs=in_specs, out_specs=out_specs, check_vma=False)
```

profile of v0, /device:TPU:0, one launch (start us, length us, event | category | flops | bytes accessed | tf_op | source)
XLA Modules:
  0.0 1910.9 jit_solution(1182851010017177751)
XLA Ops:
  10.6 56.6 %all-gather.7.cloned.1.call-done = bf16[1152,1920]{1,0:T(8,128)(2,1)} async-done(((bf16[288,1920]{1,0:T(8,128)(2,1)}), bf16[1152,1920]{1,0:T(8,128)(2,1)}) %all-gather.7.cloned.1.call-update) | async-done | bytes 4423696 | tf_op jit(solution)/shard_map/all_gather | solution.py:205
  77.2 76.4 %all-reduce.6 = (s32[3072]{0:T(1024)S(1)}, s32[3072]{0:T(1024)S(1)}) all-reduce(s32[3072]{0:T(1024)S(1)} %dynamic-update-slice, s32[3072]{0:T(1024)S(1)} %dynamic-update-slice.1), channel_id=1, replica_groups=mesh['grp'=2,'ctx'=4,'wsh'=4] {'ctx','wsh'}, use_global_device_ids=true, to_apply=%add | all-reduce | flops 6144 | bytes 49152
  168.4 31.3 %all-gather.9.cloned.1.call-done = bf16[3072,384]{1,0:T(8,128)(2,1)} async-done(((bf16[192,384]{1,0:T(8,128)(2,1)}), bf16[3072,384]{1,0:T(8,128)(2,1)}) %all-gather.9.cloned.1.call-update) | async-done | bytes 2359312 | tf_op jit(solution)/shard_map/all_gather | solution.py:226
  215.0 24.5 %while.39 = (s32[]{:T(128)}, f32[6,3,192]{2,1,0:T(4,128)S(1)}, f32[6,3,192]{2,1,0:T(4,128)S(1)}, s32[3,1024]{1,0:T(4,128)S(1)}, s32[192]{0:T(256)S(1)}, /*index=...) while((s32[]{:T(128)}, f32[6,3,192]{2,1,0:T(4,128)S(1)}, ...), condition=%wide.region_4.5_spmd.clone, body=%wide.region_1.4_spmd.clone.sunk | while | flops 482101120 | bytes 30485644 | solution.py:111
  240.2 29.6 %while.40 = (s32[]{:T(128)}, f32[192,6,3,64]{0,3,2,1:T(8,128)}, bf16[3,1024,6,64]{1,3,2,0:T(8,128)(2,1)}, s32[3,1024]{1,0:T(4,128)S(1)}, s32[192]{0:T(256)S(1)},...) while((s32[]{:T(128)}, f32[192,6,3,64]{0,3,2,1:T(8,128)}, ...), condition=%wide.region_6.7_spmd.clone, body=%wide.region_5.6_spmd.clone.sunk | while | flops 924894208 | bytes 4674702 | solution.py:132
  275.7 101.8 %all-gather.15.cloned.1.call-done = bf16[1152,6144]{1,0:T(8,128)(2,1)} async-done(((bf16[288,6144]{1,0:T(8,128)(2,1)}), bf16[1152,6144]{1,0:T(8,128)(2,1)}) %all-gather.15.cloned.1.call-update) | async-done | bytes 14155792 | tf_op jit(solution)/shard_map/all_gather | solution.py:207
  377.5 11.0 fusion.75
  388.5 67.5 %all-gather.17.cloned.1.call-done = bf16[3072,1152]{1,0:T(8,128)(2,1)} async-done(((bf16[768,1152]{1,0:T(8,128)(2,1)}), bf16[3072,1152]{1,0:T(8,128)(2,1)}) %all-gather.17.cloned.1.call-update) | async-done | bytes 7077904 | tf_op jit(solution)/shard_map/all_gather | solution.py:208
  455.9 8.8 multiply_convert_fusion.1
  464.7 11.3 multiply_reduce_fusion
  483.2 67.5 %while.41 = (s32[]{:T(128)}, f32[192,6,3,64]{0,3,2,1:T(8,128)}, f32[3,1024,6,64]{1,3,2,0:T(8,128)}, f32[3,1024,6,64]{1,3,2,0:T(8,128)}, bf16[3,1024,6,64]{1,3,2,...) while((s32[]{:T(128)}, f32[192,6,3,64]{0,3,2,1:T(8,128)}, ...), condition=%wide.region_10.11_spmd.clone, body=%wide.region_9.10_spmd.clone.sunk | while | flops 2308621312 | bytes 81001752 | solution.py:176
  556.3 9.2 copy.76
  565.5 10.3 reshape.207
  575.9 9.2 copy.77
  585.1 10.4 reshape.209
  602.1 111.3 %reduce-scatter.19.cloned.1.call-done = f32[192,384]{1,0:T(8,128)} async-done(((f32[3072,384]{1,0:T(8,128)}), f32[192,384]{1,0:T(8,128)}) %reduce-scatter.19.cloned.1.call-update) | async-done | bytes 294928
  714.5 141.3 %reduce-scatter.21.cloned.1.call-done = f32[192,384]{1,0:T(8,128)} async-done(((f32[3072,384]{1,0:T(8,128)}), f32[192,384]{1,0:T(8,128)}) %reduce-scatter.21.cloned.1.call-update) | async-done | bytes 294928
  863.0 8.6 fusion.77
  872.8 12.6 fusion.51
  886.2 115.2 %reduce-scatter.25.cloned.1.call-done = f32[72,1152]{1,0:T(8,128)} async-done(((f32[1152,1152]{1,0:T(8,128)}), f32[72,1152]{1,0:T(8,128)}) %reduce-scatter.25.cloned.1.call-update) | async-done | bytes 331792
  1003.0 170.2 %reduce-scatter.23.cloned.1.call-done = f32[72,1920]{1,0:T(8,128)} async-done(((f32[1152,1920]{1,0:T(8,128)}), f32[72,1920]{1,0:T(8,128)}) %reduce-scatter.23.cloned.1.call-update) | async-done | bytes 552976
  1175.0 224.2 %reduce-scatter.17.cloned.1.call-done = f32[192,1152]{1,0:T(8,128)} async-done(((f32[3072,1152]{1,0:T(8,128)}), f32[192,1152]{1,0:T(8,128)}) %reduce-scatter.17.cloned.1.call-update) | async-done | bytes 884752 | tf_op jit(solution)/shard_map/reduce_scatter | solution.py:305
  1401.1 403.0 %reduce-scatter.15.cloned.1.call-done = f32[72,6144]{1,0:T(8,128)} async-done(((f32[1152,6144]{1,0:T(8,128)}), f32[72,6144]{1,0:T(8,128)}) %reduce-scatter.15.cloned.1.call-update) | async-done | bytes 1769488 | tf_op jit(solution)/shard_map/reduce_scatter | solution.py:304
  1816.6 74.8 %all-reduce.7 = (bf16[1152]{0:T(1024)(128)(2,1)S(1)}, bf16[1152]{0:T(1024)(128)(2,1)S(1)}) all-reduce(f32[1152]{0:T(1024)S(1)} %get-tuple-element.388, f32[1152]{0:T(1024)S(1)} %copy-done.29), channel_id=8, replica_groups=mesh['grp'=2,'ctx'=4,'wsh'=4] {'ctx','wsh'}, use_global_device_ids=true, to_apply=%region_23.24.clone | all-reduce | flops 2304 | bytes 13824
  (236 shorter events, 229.4 us)
Async XLA Ops:
  7.2 60.0 %all-gather.7.cloned.1.call-start = ((), (), s32[]{:S(2)}) async-start(), calls=%async_computation.6 | async-start | bytes 5529600 | tf_op jit(solution)/shard_map/all_gather | solution.py:205
  7.9 146.4 %all-gather.11.cloned.1.call-start = ((), (), s32[]{:S(2)}) async-start(), calls=%async_computation.8 | async-start | bytes 2506752 | tf_op jit(solution)/shard_map/all_gather | solution.py:225
  10.6 143.4 %copy-start.14 = (f32[192,32]{0,1:T(8,128)}, f32[192,32]{0,1:T(8,128)S(1)}, u32[]{:S(2)}) copy-start(f32[192,32]{0,1:T(8,128)S(1)} %get-tuple-element.485) | copy-start | bytes 73732
  10.6 143.4 %copy-start.16 = (f32[192,32]{0,1:T(8,128)}, f32[192,32]{0,1:T(8,128)S(1)}, u32[]{:S(2)}) copy-start(f32[192,32]{0,1:T(8,128)S(1)} %get-tuple-element.486) | copy-start | bytes 73732
  72.0 127.7 %all-gather.9.cloned.1.call-start = ((), (), s32[]{:S(2)}) async-start(), calls=%async_computation.7 | async-start | bytes 2506752 | tf_op jit(solution)/shard_map/all_gather | solution.py:226
  72.8 199.3 %all-gather.13.cloned.1.call-start = ((), (), s32[]{:S(2)}) async-start(), calls=%async_computation.9 | async-start | bytes 3317760 | tf_op jit(solution)/shard_map/all_gather | solution.py:206
  73.3 304.2 %all-gather.15.cloned.1.call-start = ((), (), s32[]{:S(2)}) async-start(), calls=%async_computation.10 | async-start | bytes 17694720 | tf_op jit(solution)/shard_map/all_gather | solution.py:207
  73.9 382.0 %all-gather.17.cloned.1.call-start = ((), (), s32[]{:S(2)}) async-start(), calls=%async_computation.11 | async-start | bytes 8847360 | tf_op jit(solution)/shard_map/all_gather | solution.py:208
  74.5 638.9 %reduce-scatter.19.cloned.1.call-start = ((), (), s32[]{:S(2)}) async-start(), calls=%async_computation.14 | async-start | bytes 5013504
  269.8 118.6 %copy-start.18 = (s32[3,1024]{1,0:T(4,128)}, s32[3,1024]{1,0:T(4,128)S(1)}, u32[]{:S(2)}) copy-start(s32[3,1024]{1,0:T(4,128)S(1)} %get-tuple-element.899) | copy-start | bytes 36868
  269.8 118.6 %copy-start.20 = (s32[192]{0:T(256)}, s32[192]{0:T(256)S(1)}, u32[]{:S(2)}) copy-start(s32[192]{0:T(256)S(1)} %get-tuple-element.902) | copy-start | bytes 2308
  269.8 107.7 %copy-start.21 = (f32[1152]{0:T(1024)S(1)}, f32[1152]{0:T(1024)}, u32[]{:S(2)}) copy-start(f32[1152]{0:T(1024)} %param.22) | copy-start | bytes 13828
  275.7 200.3 %copy-start.24 = (f32[192]{0:T(256)}, f32[192]{0:T(256)S(1)}, u32[]{:S(2)}) copy-start(f32[192]{0:T(256)S(1)} %get-tuple-element.490) | copy-start | bytes 2308
  377.5 78.4 %copy-start.11 = (bf16[192,1152]{1,0:T(8,128)(2,1)S(1)}, bf16[192,1152]{1,0:T(8,128)(2,1)}, u32[]{:S(2)}) copy-start(bf16[192,1152]{1,0:T(8,128)(2,1)} %param.25) | copy-start | bytes 1327108
  575.9 279.9 %reduce-scatter.21.cloned.1.call-start = ((), (), s32[]{:S(2)}) async-start(), calls=%async_computation.15 | async-start | bytes 5013504
  595.6 405.8 %reduce-scatter.25.cloned.1.call-start = ((), (), s32[]{:S(2)}) async-start(), calls=%async_computation.17 | async-start | bytes 5640192
  600.2 573.0 %reduce-scatter.23.cloned.1.call-start = ((), (), s32[]{:S(2)}) async-start(), calls=%async_computation.16 | async-start | bytes 9400320
  601.6 255.4 %copy-start.8 = (bf16[192,1152]{1,0:T(8,128)(2,1)S(1)}, bf16[192,1152]{1,0:T(8,128)(2,1)}, u32[]{:S(2)}) copy-start(bf16[192,1152]{1,0:T(8,128)(2,1)} %param.16) | copy-start | bytes 1327108
  601.6 255.4 %copy-start.23 = (f32[1152]{0:T(1024)S(1)}, f32[1152]{0:T(1024)}, u32[]{:S(2)}) copy-start(f32[1152]{0:T(1024)} %param.19) | copy-start | bytes 13828
  601.6 255.4 %copy-start.27 = (f32[192]{0:T(256)S(1)}, f32[192]{0:T(256)}, u32[]{:S(2)}) copy-start(f32[192]{0:T(256)} %copy-done.26) | copy-start | bytes 2308
  862.1 537.1 %reduce-scatter.17.cloned.1.call-start = ((), (), s32[]{:S(2)}) async-start(), calls=%async_computation.13 | async-start | bytes 15040512 | tf_op jit(solution)/shard_map/reduce_scatter | solution.py:305
  871.7 932.5 %reduce-scatter.15.cloned.1.call-start = ((), (), s32[]{:S(2)}) async-start(), calls=%async_computation.12 | async-start | bytes 30081024 | tf_op jit(solution)/shard_map/reduce_scatter | solution.py:304
  885.4 1010.8 %all-reduce.12.cloned.1.call-start = ((), (), s32[]{:S(2)}) async-start(), calls=%async_computation.18 | async-start | bytes 3538944 | tf_op jit(solution)/shard_map/psum | solution.py:310
  1812.5 82.5 %copy-start.30 = (f32[192]{0:T(256)S(1)}, f32[192]{0:T(256)}, u32[]{:S(2)}) copy-start(f32[192]{0:T(256)} %get-tuple-element.487) | copy-start | bytes 2308
  (27 other events, 187.7 us)
Sparse Core Ops, SparseCore 0:
  9.8 57.3 all-gather.6
  72.1 62.8 all-gather.10
  138.4 61.2 all-gather.8
  201.4 38.7 all-gather.12
  241.9 135.5 all-gather.14
  379.2 76.6 all-gather.16
  576.0 137.3 reduce-scatter.18
  719.4 136.3 reduce-scatter.20
  861.1 140.2 reduce-scatter.24
  1006.9 166.2 reduce-scatter.22
  1179.0 220.1 reduce-scatter.16
  1405.8 398.3 reduce-scatter.14
  1807.4 19.9 all-reduce.11
where the time goes:
time: 1920 us; the launch traced here: 1910 us
  waiting for transfers between devices  1420 us (74%)
  matrix products  173 us (9%)
  blocking collectives  154 us (8%)
  local copies, waits for them, and re-layouts  82.4 us (4%)
  other arithmetic  59.4 us (3%)
    unnamed x17, waiting for transfers between devices  540 us
    reduce_scatter x1, waiting for transfers between devices, local(): lax.psum_scatter(gate_up_grad, ('ctx', 'wsh'), scatter_dimension=0, tiled...  403 us
    reduce_scatter x1, waiting for transfers between devices, local(): lax.psum_scatter(down_grad, ('ctx', 'wsh'), scatter_dimension=0, tiled=True)  224 us
    unnamed x2, blocking collectives  151 us
    all_gather x1, waiting for transfers between devices, local(): lax.all_gather(gate_up, 'wsh', axis=0, tiled=True)  102 us
    all_gather x1, waiting for transfers between devices, local(): lax.all_gather(down_weight, 'wsh', axis=0, tiled=True)  67.5 us
    unnamed x73, local copies, waits for them, and re-layouts  62.7 us
    all_gather x1, waiting for transfers between devices, local(): lax.all_gather(query_key_value, 'wsh', axis=0, tiled=True)  56.6 us
  transfers between devices with their start and end apart: 13, of which 10 were waited for; matrix products, arithmetic and copies ran while one was open for 9% of the time, Pallas kernels for 0%

commit v1 on v0

--- a/solution.py
+++ b/solution.py
@@ -12,6 +12,18 @@
 QW = 1152
 KW = 384
 EPSILON = 1e-05
+
+
+def doubled_up(x, axis, dim):
+    ways, here = (lax.axis_size(axis), lax.axis_index(axis))
+    grown, reach = (x, 1)
+    while reach < ways:
+        theirs = lax.ppermute(grown, axis, [(d, d ^ reach) for d in range(ways)])
+        mine_first = jnp.concatenate([grown, theirs], axis=dim)
+        theirs_first = jnp.concatenate([theirs, grown], axis=dim)
+        grown = jnp.where(here & reach == 0, mine_first, theirs_first)
+        reach = 2 * reach
+    return grown
 
 
 def rope_angles(positions):
@@ -204,7 +216,7 @@
     full_qkv, full_out, full_gate_up, full_down = (
         lax.all_gather(query_key_value, "wsh", axis=0, tiled=True),
         lax.all_gather(attend_out, "wsh", axis=0, tiled=True),
-        lax.all_gather(gate_up, "wsh", axis=0, tiled=True),
+        doubled_up(gate_up, "wsh", 0),
         lax.all_gather(down_weight, "wsh", axis=0, tiled=True),
     )
     projected = jnp.dot(normed_one, full_qkv, preferred_element_type=jnp.float32)

time: 1920 us -> 2060 us (1.073)
  blocking collectives: 154 us -> 232 us
  matrix products: 173 us -> 216 us
    ppermute x0 -> x2, waiting for transfers between devices: none -> 143 us  [doubled_up(): theirs = lax.ppermute(grown, axis, [(d, d ^ reach) for d in range(ways)])]
    unnamed x2, blocking collectives: 151 us -> 229 us
    all_gather x1, waiting for transfers between devices: 67.5 us -> 0.01 us  [local(): lax.all_gather(down_weight, 'wsh', axis=0, tiled=True)]
    all_gather x1, waiting for transfers between devices: 102 us -> 52.1 us  [local(): lax.all_gather(gate_up, 'wsh', axis=0, tiled=True)]
    all_gather x1, waiting for transfers between devices: 31.3 us -> 0.02 us  [local(): lax.all_gather(value_local, ('ctx', 'wsh'), axis=0, tiled=True)]
    unnamed x73 -> x81, local copies, waits for them, and re-layouts: 62.7 us -> 66.3 us
  transfers between devices with their start and end apart: 13 -> 15, of which waited for: 10 -> 9; matrix products, arithmetic and copies ran while one was open for 9% -> 11% of each run, Pallas kernels for 0% -> 0%
where the time goes in v1:
time: 2060 us; the launch traced here: 2050 us
  waiting for transfers between devices  1420 us (69%)
  blocking collectives  232 us (11%)
  matrix products  216 us (10%)
  local copies, waits for them, and re-layouts  92.8 us (5%)
  other arithmetic  71.4 us (3%)
    unnamed x17, waiting for transfers between devices  542 us
    reduce_scatter x1, waiting for transfers between devices, local(): lax.psum_scatter(gate_up_grad, ('ctx', 'wsh'), scatter_dimension=0, tiled...  402 us
    unnamed x2, blocking collectives  229 us
    reduce_scatter x1, waiting for transfers between devices, local(): lax.psum_scatter(down_grad, ('ctx', 'wsh'), scatter_dimension=0, tiled=True)  224 us
    ppermute x2, waiting for transfers between devices, doubled_up(): theirs = lax.ppermute(grown, axis, [(d, d ^ reach) for d in range(ways)])  143 us
    unnamed x81, local copies, waits for them, and re-layouts  66.3 us
    all_gather x1, waiting for transfers between devices, local(): lax.all_gather(query_key_value, 'wsh', axis=0, tiled=True)  55.9 us
    all_gather x1, waiting for transfers between devices, local(): lax.all_gather(gate_up, 'wsh', axis=0, tiled=True)  52.1 us
  transfers between devices with their start and end apart: 15, of which 9 were waited for; matrix products, arithmetic and copies ran while one was open for 11% of the time, Pallas kernels for 0%

profile of v1, /device:TPU:0, one launch (start us, length us, event | category | flops | bytes accessed | tf_op | source)
XLA Modules:
  0.0 2049.8 jit_solution(8635507766335848485)
XLA Ops:
  11.3 55.9 %all-gather.7.cloned.1.call-done = bf16[1152,1920]{1,0:T(8,128)(2,1)} async-done(((bf16[288,1920]{1,0:T(8,128)(2,1)}), bf16[1152,1920]{1,0:T(8,128)(2,1)}) %all-gather.7.cloned.1.call-update) | async-done | bytes 4423696 | tf_op jit(solution)/shard_map/all_gather | solution.py:217
  89.0 154.4 %all-reduce.6 = (s32[3072]{0:T(1024)}, s32[3072]{0:T(1024)}) all-reduce(s32[3072]{0:T(1024)} %dynamic-update-slice, s32[3072]{0:T(1024)} %dynamic-update-slice.1), channel_id=1, replica_groups=mesh['grp'=2,'ctx'=4,'wsh'=4] {'ctx','wsh'}, use_global_device_ids=true, to_apply=%add | all-reduce | flops 6144 | bytes 49152
  268.8 43.5 %while.39 = (s32[]{:T(128)}, f32[6,3,192]{2,1,0:T(4,128)S(1)}, f32[6,3,192]{2,1,0:T(4,128)S(1)}, s32[3,1024]{1,0:T(4,128)S(1)}, s32[192]{0:T(256)S(1)}, /*index=...) while((s32[]{:T(128)}, f32[6,3,192]{2,1,0:T(4,128)S(1)}, ...), condition=%wide.region_4.5_spmd.clone, body=%wide.region_1.4_spmd.clone.sunk | while | flops 482101120 | bytes 30485644 | solution.py:123
  327.8 27.4 %while.40 = (s32[]{:T(128)}, f32[192,6,3,64]{0,3,2,1:T(8,128)}, bf16[3,1024,6,64]{1,3,2,0:T(8,128)(2,1)}, s32[3,1024]{1,0:T(4,128)S(1)}, s32[192]{0:T(256)S(1)},...) while((s32[]{:T(128)}, f32[192,6,3,64]{0,3,2,1:T(8,128)}, ...), condition=%wide.region_6.7_spmd.clone, body=%wide.region_5.6_spmd.clone.sunk | while | flops 924894208 | bytes 4674702 | solution.py:144
  361.1 142.7 %collective-permute-done.1 = bf16[576,6144]{1,0:T(8,128)(2,1)} collective-permute-done((bf16[576,6144]{1,0:T(8,128)(2,1)}, bf16[576,6144]{1,0:T(8,128)(2,1)}, u32[]{:S(2)}, u32[]{:S(2)}) %collective-permute-start.1) | collective-permute-done | bytes 7077920 | tf_op jit(solution)/shard_map/ppermute | solution.py:21
  503.8 13.7 fusion.49
  526.5 52.1 %all-gather.17.cloned.1.call-done = bf16[1152,6144]{1,0:T(8,128)(2,1)} async-done(((bf16[288,6144]{1,0:T(8,128)(2,1)}), bf16[1152,6144]{1,0:T(8,128)(2,1)}) %all-gather.17.cloned.1.call-update) | async-done | bytes 14155792 | tf_op jit(solution)/shard_map/all_gather | solution.py:261
  578.6 12.3 multiply_reduce_fusion
  597.3 92.4 %while.41 = (s32[]{:T(128)}, f32[192,6,3,64]{0,3,2,1:T(8,128)}, f32[3,1024,6,64]{1,3,2,0:T(8,128)}, f32[3,1024,6,64]{1,3,2,0:T(8,128)}, bf16[3,1024,6,64]{1,3,2,...) while((s32[]{:T(128)}, f32[192,6,3,64]{0,3,2,1:T(8,128)}, ...), condition=%wide.region_10.11_spmd.clone, body=%wide.region_9.10_spmd.clone.sunk | while | flops 2308621312 | bytes 187093232 | solution.py:188
  600.1 9.6 fusion.144
  630.6 9.6 fusion.144
  661.4 9.6 fusion.144
  695.1 9.2 copy.76
  704.4 10.3 reshape.207
  714.8 9.2 copy.77
  724.0 10.4 reshape.209
  749.7 102.1 %reduce-scatter.19.cloned.1.call-done = f32[192,384]{1,0:T(8,128)} async-done(((f32[3072,384]{1,0:T(8,128)}), f32[192,384]{1,0:T(8,128)}) %reduce-scatter.19.cloned.1.call-update) | async-done | bytes 294928
  853.0 141.6 %reduce-scatter.21.cloned.1.call-done = f32[192,384]{1,0:T(8,128)} async-done(((f32[3072,384]{1,0:T(8,128)}), f32[192,384]{1,0:T(8,128)}) %reduce-scatter.21.cloned.1.call-update) | async-done | bytes 294928
  1002.1 12.5 fusion.58
  1015.2 124.5 %reduce-scatter.25.cloned.1.call-done = f32[72,1152]{1,0:T(8,128)} async-done(((f32[1152,1152]{1,0:T(8,128)}), f32[72,1152]{1,0:T(8,128)}) %reduce-scatter.25.cloned.1.call-update) | async-done | bytes 331792
  1141.4 224.2 %reduce-scatter.17.cloned.1.call-done = f32[192,1152]{1,0:T(8,128)} async-done(((f32[3072,1152]{1,0:T(8,128)}), f32[192,1152]{1,0:T(8,128)}) %reduce-scatter.17.cloned.1.call-update) | async-done | bytes 884752 | tf_op jit(solution)/shard_map/reduce_scatter | solution.py:317
  1367.5 171.6 %reduce-scatter.23.cloned.1.call-done = f32[72,1920]{1,0:T(8,128)} async-done(((f32[1152,1920]{1,0:T(8,128)}), f32[72,1920]{1,0:T(8,128)}) %reduce-scatter.23.cloned.1.call-update) | async-done | bytes 552976
  1540.9 402.2 %reduce-scatter.15.cloned.1.call-done = f32[72,6144]{1,0:T(8,128)} async-done(((f32[1152,6144]{1,0:T(8,128)}), f32[72,6144]{1,0:T(8,128)}) %reduce-scatter.15.cloned.1.call-update) | async-done | bytes 1769488 | tf_op jit(solution)/shard_map/reduce_scatter | solution.py:316
  1955.5 74.7 %all-reduce.7 = (bf16[1152]{0:T(1024)(128)(2,1)S(1)}, bf16[1152]{0:T(1024)(128)(2,1)S(1)}) all-reduce(f32[1152]{0:T(1024)S(1)} %get-tuple-element.388, f32[1152]{0:T(1024)S(1)} %copy-done.32), channel_id=8, replica_groups=mesh['grp'=2,'ctx'=4,'wsh'=4] {'ctx','wsh'}, use_global_device_ids=true, to_apply=%region_23.24.clone | all-reduce | flops 2304 | bytes 13824
  (243 shorter events, 280.7 us)
Async XLA Ops:
  7.2 60.0 %all-gather.7.cloned.1.call-start = ((), (), s32[]{:S(2)}) async-start(), calls=%async_computation.6 | async-start | bytes 5529600 | tf_op jit(solution)/shard_map/all_gather | solution.py:217
  7.9 246.6 %all-gather.11.cloned.1.call-start = ((), (), s32[]{:S(2)}) async-start(), calls=%async_computation.8 | async-start | bytes 2506752 | tf_op jit(solution)/shard_map/all_gather | solution.py:237
  10.4 56.8 %copy-start.28 = (f32[192]{0:T(256)}, f32[192]{0:T(256)S(1)}, u32[]{:S(2)}) copy-start(f32[192]{0:T(256)S(1)} %get-tuple-element.488) | copy-start | bytes 2308
  72.0 15.6 copy-start.23
  78.6 233.8 %all-gather.9.cloned.1.call-start = ((), (), s32[]{:S(2)}) async-start(), calls=%async_computation.7 | async-start | bytes 2506752 | tf_op jit(solution)/shard_map/all_gather | solution.py:238
  80.3 277.0 %all-gather.13.cloned.1.call-start = ((), (), s32[]{:S(2)}) async-start(), calls=%async_computation.9 | async-start | bytes 3317760 | tf_op jit(solution)/shard_map/all_gather | solution.py:218
  80.9 436.6 %all-gather.15.cloned.1.call-start = ((), (), s32[]{:S(2)}) async-start(), calls=%async_computation.10 | async-start | bytes 8847360 | tf_op jit(solution)/shard_map/all_gather | solution.py:220
  81.5 497.1 %all-gather.17.cloned.1.call-start = ((), (), s32[]{:S(2)}) async-start(), calls=%async_computation.11 | async-start | bytes 17694720 | tf_op jit(solution)/shard_map/all_gather | solution.py:261
  82.1 769.8 %reduce-scatter.19.cloned.1.call-start = ((), (), s32[]{:S(2)}) async-start(), calls=%async_computation.14 | async-start | bytes 5013504
  82.1 163.4 %collective-permute-start = (bf16[288,6144]{1,0:T(8,128)(2,1)S(1)}, bf16[288,6144]{1,0:T(8,128)(2,1)}, u32[]{:S(2)}, u32[]{:S(2)}) collective-permute-start(bf16[288,6144]{1,0:T(8,128)(2,1)S(1)} %copy-done.3), channel_id=1, source_target_pairs={{0,1},{1,0},{2,3},{3,2},{4,5},{5,4},{6,7},{7,6},{8,9},{9,8},{10,11... | collective-permute-start | bytes 10616840 | tf_op jit(solution)/shard_map/ppermute | solution.py:21
  252.9 250.9 %collective-permute-start.1 = (bf16[576,6144]{1,0:T(8,128)(2,1)}, bf16[576,6144]{1,0:T(8,128)(2,1)}, u32[]{:S(2)}, u32[]{:S(2)}) collective-permute-start(bf16[576,6144]{1,0:T(8,128)(2,1)} %maximum_select_fusion.2), channel_id=1, source_target_pairs={{0,2},{1,3},{2,0},{3,1},{4,6},{5,7},{6,4},{7,5},{8,10},{9,11},{10,... | collective-permute-start | bytes 21233672 | tf_op jit(solution)/shard_map/ppermute | solution.py:21
  327.8 29.6 %copy-start.6 = (bf16[192,1152]{1,0:T(8,128)(2,1)S(1)}, bf16[192,1152]{1,0:T(8,128)(2,1)}, u32[]{:S(2)}) copy-start(bf16[192,1152]{1,0:T(8,128)(2,1)} %param.16) | copy-start | bytes 1327108
  355.1 148.7 %copy-start.26 = (f32[1152]{0:T(1024)S(1)}, f32[1152]{0:T(1024)}, u32[]{:S(2)}) copy-start(f32[1152]{0:T(1024)} %param.22) | copy-start | bytes 13828
  361.1 229.9 %copy-start.30 = (f32[192]{0:T(256)}, f32[192]{0:T(256)S(1)}, u32[]{:S(2)}) copy-start(f32[192]{0:T(256)S(1)} %get-tuple-element.490) | copy-start | bytes 2308
  714.7 279.9 %reduce-scatter.21.cloned.1.call-start = ((), (), s32[]{:S(2)}) async-start(), calls=%async_computation.15 | async-start | bytes 5013504
  734.4 405.2 %reduce-scatter.25.cloned.1.call-start = ((), (), s32[]{:S(2)}) async-start(), calls=%async_computation.17 | async-start | bytes 5640192
  739.2 626.4 %reduce-scatter.17.cloned.1.call-start = ((), (), s32[]{:S(2)}) async-start(), calls=%async_computation.13 | async-start | bytes 15040512 | tf_op jit(solution)/shard_map/reduce_scatter | solution.py:317
  747.9 248.0 %copy-start.7 = (bf16[192,1152]{1,0:T(8,128)(2,1)S(1)}, bf16[192,1152]{1,0:T(8,128)(2,1)}, u32[]{:S(2)}) copy-start(bf16[192,1152]{1,0:T(8,128)(2,1)} %param.16) | copy-start | bytes 1327108
  747.9 247.9 %copy-start.25 = (f32[1152]{0:T(1024)S(1)}, f32[1152]{0:T(1024)}, u32[]{:S(2)}) copy-start(f32[1152]{0:T(1024)} %param.19) | copy-start | bytes 13828
  747.9 247.9 %copy-start.29 = (f32[192]{0:T(256)S(1)}, f32[192]{0:T(256)}, u32[]{:S(2)}) copy-start(f32[192]{0:T(256)} %copy-done.28) | copy-start | bytes 2308
  747.9 791.2 %reduce-scatter.23.cloned.1.call-start = ((), (), s32[]{:S(2)}) async-start(), calls=%async_computation.16 | async-start | bytes 9400320
  1000.9 942.1 %reduce-scatter.15.cloned.1.call-start = ((), (), s32[]{:S(2)}) async-start(), calls=%async_computation.12 | async-start | bytes 30081024 | tf_op jit(solution)/shard_map/reduce_scatter | solution.py:316
  1014.5 1020.5 %all-reduce.12.cloned.1.call-start = ((), (), s32[]{:S(2)}) async-start(), calls=%async_computation.18 | async-start | bytes 3538944 | tf_op jit(solution)/shard_map/psum | solution.py:322
  1951.4 82.5 %copy-start.33 = (f32[192]{0:T(256)S(1)}, f32[192]{0:T(256)}, u32[]{:S(2)}) copy-start(f32[192]{0:T(256)} %get-tuple-element.487) | copy-start | bytes 2308
  (30 other events, 187.9 us)
Sparse Core Ops, SparseCore 0:
  9.8 57.3 all-gather.6
  78.7 73.8 all-gather.10
  156.0 61.8 all-gather.8
  219.6 50.4 all-gather.12
  271.7 136.6 all-gather.14
  410.1 168.4 all-gather.16
  714.9 136.9 reduce-scatter.18
  857.8 136.7 reduce-scatter.20
  999.9 139.7 reduce-scatter.24
  1145.3 220.1 reduce-scatter.16
  1372.2 166.8 reduce-scatter.22
  1545.7 397.3 reduce-scatter.14
  1946.4 19.9 all-reduce.11
